TPU v7x, 256 devices: a whole 4x4x8 slice. The times are simulated.
256 devices in a mesh: dp: 32 (over z, y), seq: 8 (over x, core).
Axes of the slice: x: 4, y: 4, z: 8, core: 2. Of those that a mesh axis runs over, the one named last changes fastest.
Arguments:
- prefill_queries: bfloat16 [32768, 4096], P(('dp', 'seq')), may hold values from -8 to 8
- prefill_key_values: bfloat16 [32768, 2048], P(('dp', 'seq')), may hold values from -8 to 8
- decode_queries: bfloat16 [32, 4096], P('dp', 'seq'), may hold values from -8 to 8
- decode_key_values: bfloat16 [32, 2048], P('dp', 'seq'), may hold values from -8 to 8
- arrival: int32 [32], replicated, may hold values from 0 to 31, as said below
- pooled_key_values: bfloat16 [1024, 128, 2048], P('dp', None, 'seq'), may hold values from -8 to 8
- page_table: int32 [32, 32], P('dp'), may hold values from 0 to 31, as said below
- cache_len: int32 [32], P('dp'), may hold values from 1 to 4096, as said below
- mover: int32 [32], P('dp'), may hold values from 0 to 0, as said below
Outputs:
- prefill_out: bfloat16 [32768, 4096], P(('dp', 'seq'))
- decode_out: bfloat16 [32, 4096], P('dp', 'seq')
- received_pages: bfloat16 [1024, 128, 2048], P('dp', None, 'seq')
Inputs may be any that keep to these rules, and one draw needn't show every extreme that they name: `arrival`: every decode request appears exactly once. `page_table`: the 1 request of one group together name each of that group's 32 pages exactly once. `cache_len`: some request has exactly 4096 cached tokens in every draw. `mover`: the request with the most cached tokens always moves.
All inputs are finite; a program needn't handle non-finite values.
Results may differ from a plain program's by a relative error of at most 0.006.
Values may be sent and summed in bfloat16 or wider, within the bound.
A program may use at most 64 MiB of HBM per device.

v0:
```python
import math
import jax
import jax.numpy as jnp
from jax import lax
from jax.sharding import PartitionSpec as P

QUERY_HEADS = 32
KV_HEAD_COUNT = 8
HEAD_SIZE = 128
NEG_FILL = -1e30


def passed_along(block, axis, distance):
    devices = range(lax.axis_size(axis))
    route = [((i - distance) % len(devices), i) for i in devices]
    return lax.ppermute(block, axis, route)


def keys_attention(prefill_queries, prefill_key_values):
    group_local_rows = prefill_queries.shape[0]
    group_extent = QUERY_HEADS // KV_HEAD_COUNT
    query_rows = prefill_queries.reshape(group_local_rows, KV_HEAD_COUNT, group_extent, HEAD_SIZE)
    row_offset = lax.axis_index("seq") * group_local_rows
    scale_factor = 1.0 / math.sqrt(HEAD_SIZE)
    query_pos = row_offset + lax.broadcasted_iota(jnp.int32, (group_local_rows, 1), 0)
    state_dimensions = (KV_HEAD_COUNT, group_extent, group_local_rows)
    portion_slice = lax.all_gather(prefill_key_values, "seq", axis=0, tiled=True)
    first_index = jnp.int32(0)
    run_max = jnp.full(state_dimensions, NEG_FILL, jnp.float32)
    run_total = jnp.zeros(state_dimensions, jnp.float32)
    run_acc = jnp.zeros(state_dimensions + (HEAD_SIZE,), jnp.float32)
    portion_rows = portion_slice.shape[0]
    key_value_rows = portion_slice.reshape(portion_rows, KV_HEAD_COUNT, 2 * HEAD_SIZE)
    for first_key in range(0, portion_rows, 512):
        width_now = min(512, portion_rows - first_key)
        key_block = key_value_rows[first_key : first_key + width_now]
        scores = (
            jnp.einsum(
                "qngd,knd->ngqk",
                query_rows,
                key_block[:, :, :HEAD_SIZE],
                preferred_element_type=jnp.float32,
            )
            * scale_factor
        )
        key_pos = first_index + first_key + lax.broadcasted_iota(jnp.int32, (1, width_now), 1)
        allowed = key_pos <= query_pos
        masked = jnp.where(allowed, scores, NEG_FILL)
        new_max = jnp.maximum(run_max, jnp.max(masked, axis=-1))
        rescale = jnp.exp(run_max - new_max)
        weights = jnp.where(allowed, jnp.exp(masked - new_max[..., None]), 0.0).astype(jnp.bfloat16)
        run_total = run_total * rescale + jnp.sum(weights, axis=-1, dtype=jnp.float32)
        run_acc = run_acc * rescale[..., None] + jnp.einsum(
            "ngqk,knd->ngqd",
            weights,
            key_block[:, :, HEAD_SIZE:],
            preferred_element_type=jnp.float32,
        )
        run_max = new_max
    normed = run_acc / run_total[..., None]
    return (
        jnp.transpose(normed, (2, 0, 1, 3))
        .astype(jnp.bfloat16)
        .reshape(group_local_rows, QUERY_HEADS * HEAD_SIZE)
    )


def decode_attention(
    decode_queries, decode_key_values, arrival, pooled_key_values, page_table, cache_len
):
    request_count = decode_queries.shape[0]
    kv_local = decode_key_values.shape[1] // (2 * HEAD_SIZE)
    group_extent = QUERY_HEADS // KV_HEAD_COUNT
    query_all, pair_all = (
        lax.all_gather(decode_queries, "dp", axis=0, tiled=True),
        lax.all_gather(decode_key_values, "dp", axis=0, tiled=True),
    )
    total_rows = query_all.shape[0]
    wanted = lax.axis_index("dp") * request_count + lax.broadcasted_iota(
        jnp.int32, (request_count, 1), 0
    )
    row_ids = lax.broadcasted_iota(jnp.int32, (request_count, total_rows), 1)
    decode_row = jnp.sum(jnp.where(arrival[None, :] == wanted, row_ids, 0), axis=1)
    query_sel = jnp.take(query_all, decode_row, axis=0).reshape(
        request_count, kv_local, group_extent, HEAD_SIZE
    )
    pair_sel = jnp.take(pair_all, decode_row, axis=0).reshape(
        request_count, kv_local, 2 * HEAD_SIZE
    )
    cache_row_list = jnp.take(pooled_key_values, page_table, axis=0)
    cache_row_list = cache_row_list.reshape(request_count, -1, kv_local, 2 * HEAD_SIZE)
    span_rows = cache_row_list.shape[1]
    scale_factor = 1.0 / math.sqrt(HEAD_SIZE)
    cached_scores = (
        jnp.einsum(
            "rngd,rtnd->rngt",
            query_sel,
            cache_row_list[..., :HEAD_SIZE],
            preferred_element_type=jnp.float32,
        )
        * scale_factor
    )
    new_scores = (
        jnp.einsum(
            "rngd,rnd->rng",
            query_sel,
            pair_sel[..., :HEAD_SIZE],
            preferred_element_type=jnp.float32,
        )
        * scale_factor
    )
    valid_rows = (
        lax.broadcasted_iota(jnp.int32, (request_count, 1, 1, span_rows), 3)
        < cache_len[:, None, None, None]
    )
    masked = jnp.where(valid_rows, cached_scores, NEG_FILL)
    row_max = jnp.maximum(jnp.max(masked, axis=-1), new_scores)
    cached_weights = jnp.where(valid_rows, jnp.exp(masked - row_max[..., None]), 0.0).astype(
        jnp.bfloat16
    )
    new_weights = jnp.exp(new_scores - row_max).astype(jnp.bfloat16)
    wide_new = new_weights.astype(jnp.float32)
    totals = jnp.sum(cached_weights, axis=-1, dtype=jnp.float32) + wide_new
    summed = jnp.einsum(
        "rngt,rtnd->rngd",
        cached_weights,
        cache_row_list[..., HEAD_SIZE:],
        preferred_element_type=jnp.float32,
    )
    summed = (
        summed + wide_new[..., None] * pair_sel[..., HEAD_SIZE:].astype(jnp.float32)[:, :, None, :]
    )
    return (
        (summed / totals[..., None])
        .astype(jnp.bfloat16)
        .reshape(request_count, kv_local * group_extent * HEAD_SIZE)
    )


def move_pages(pooled_key_values, page_table, cache_len, mover):
    mover_slot = mover[0]
    moving_table = lax.dynamic_index_in_dim(page_table, mover_slot, 0, keepdims=False)
    moving_len = lax.dynamic_index_in_dim(cache_len, mover_slot, 0, keepdims=False)
    page_rows = jnp.take(pooled_key_values, moving_table, axis=0)
    live_pages = (
        lax.broadcasted_iota(jnp.int32, (page_rows.shape[0], 1, 1), 0) * page_rows.shape[1]
        < moving_len
    )
    page_rows = jnp.where(live_pages, page_rows, jnp.zeros_like(page_rows))
    return passed_along(page_rows, "dp", 1)


def on_device(
    prefill_queries,
    prefill_key_values,
    decode_queries,
    decode_key_values,
    arrival,
    pooled_key_values,
    page_table,
    cache_len,
    mover,
):
    prefill_out = keys_attention(prefill_queries, prefill_key_values)
    decode_out = decode_attention(
        decode_queries, decode_key_values, arrival, pooled_key_values, page_table, cache_len
    )
    received_pages = move_pages(pooled_key_values, page_table, cache_len, mover)
    return (prefill_out, decode_out, received_pages)


def solution(mesh):
    placed = (
        P(("dp", "seq"), None),
        P(("dp", "seq"), None),
        P("dp", "seq"),
        P("dp", "seq"),
        P(),
        P("dp", None, "seq"),
        P("dp", None),
        P("dp"),
        P("dp"),
    )
    return jax.shard_map(
        on_device,
        mesh=mesh,
        in_specs=placed,
        out_specs=(P(("dp", "seq"), None), P("dp", "seq"), P("dp", None, "seq")),
        check_vma=False,
    )
```

profile of v0, /device:TPU:6, one launch (start us, length us, event | category | flops | bytes accessed | tf_op | source)
XLA Modules:
  0.0 181.2 jit_solution(11569675293962441517)
XLA Ops:
  7.2 2.2 %copy.26 = bf16[128,2048]{0,1:T(8,128)(2,1)} copy(bf16[128,2048]{1,0:T(8,128)(2,1)} %param.10) | data formatting | bytes 1048576 | tf_op args[1]
  10.1 0.7 fusion.23
  10.8 2.0 %gather_fusion.1 = bf16[32,128,256]{2,1,0:T(8,128)(2,1)} fusion(bf16[32,128,256]{2,1,0:T(8,128)(2,1)S(1)} %copy-done, s32[1024]{0:T(1024)S(1)} %pad_clamp_fusion), kind=kCustom, calls=%fused_computation.1 | custom fusion | bytes 4194432 | tf_op jit(solution)/shard_map/jit(_take)/gather | solution.py:144
  12.8 3.3 %select_select_fusion = bf16[32,128,256]{2,1,0:T(8,128)(2,1)} fusion(bf16[32,128,256]{2,1,0:T(8,128)(2,1)} %gather_fusion.1, pred[32]{0:T(512)(128)(4,1)S(1)} %get-tuple-element.57, pred[32]{0:T(512)(128)(4,1)S(1)} %get-tuple-element.58), kind=kLoop, calls=%fused_computation.17 | loop fusion | flops 2097152 | bytes 4194368 | tf_op jit(solution)/shard_map/jit(_where)/select_n | solution.py:149
  16.0 1.6 collective-permute-start
  17.6 1.8 reshape.261
  19.5 2.0 %gather_fusion = bf16[32,128,256]{2,1,0:T(8,128)(2,1)} fusion(bf16[32,128,256]{2,1,0:T(8,128)(2,1)S(1)} %copy-done, s32[1024]{0:T(1024)S(1)} %pad_clamp_fusion.1), kind=kCustom, calls=%fused_computation | custom fusion | bytes 4194432 | tf_op jit(solution)/shard_map/jit(_take)/gather | solution.py:90
  21.6 1.9 %broadcast_select_fusion = bf16[1,4096,1,256]{3,1,2,0:T(8,128)(2,1)S(1)} fusion(bf16[1,4096,1,256]{3,1,2,0:T(8,128)(2,1)} %bitcast.141, pred[4096]{0:T(1024)(128)(4,1)S(1)} %broadcast_bitcast_fusion), kind=kLoop, calls=%fused_computation.18 | loop fusion | flops 1048576 | bytes 4198400 | tf_op jit(solution)/shard_map/jit(_take)/select_n | solution.py:90
  23.5 0.6 fusion.22
  26.1 84.3 %all-gather = bf16[32,1,512]{2,1,0:T(2,128)(2,1)S(1)} all-gather(bf16[1,1,512]{2,1,0:T(2,128)(2,1)S(1)} %bitcast.147), channel_id=1, replica_groups=mesh['dp'=32,'seq'=8] {'dp'}, dimensions={0}, use_global_device_ids=true | all-gather | bytes 33792 | tf_op jit(solution)/shard_map/all_gather | solution.py:75
  110.4 41.7 %all-gather.1 = bf16[32,1,256]{2,1,0:T(2,128)(2,1)S(1)} all-gather(bf16[1,1,256]{2,1,0:T(2,128)(2,1)S(1)} %bitcast.149), channel_id=1, replica_groups=mesh['dp'=32,'seq'=8] {'dp'}, dimensions={0}, use_global_device_ids=true | all-gather | bytes 16896 | tf_op jit(solution)/shard_map/all_gather | solution.py:76
  152.2 0.5 fusion.30
  152.8 0.2 convert_reduce_fusion.2
  153.0 0.3 fusion.8
  153.3 0.6 copy.52
  153.9 0.1 broadcast_compare_fusion
  154.1 2.5 %fusion.29 = (bf16[512,2048]{0,1:T(8,128)(2,1)S(1)}, bf16[512,2048]{0,1:T(8,128)(2,1)S(1)}) fusion(bf16[1024,2048]{0,1:T(8,128)(2,1)} %all-gather.4.cloned.1.call-done), kind=kLoop, calls=%fused_computation.77 | loop fusion | bytes 8388608 | tf_op jit(solution)/shard_map/slice | solution.py:36
  156.6 2.1 %fusion = (f32[8,4,128]{2,1,0:T(4,128)S(1)}, f32[8,512,128,4]{2,1,3,0:T(8,128)S(1)}) fusion(pred[128,512]{0,1:T(8,128)(4,1)S(1)} %get-tuple-element.46, bf16[128,8,4,128]{3,2,1,0:T(4,128)(2,1)S(1)} %reshape.261, bf16[512,8,256]{0,2,1:T(8,128)(2,1)S(1)} %bitcast.144), kind=kOutput, calls=%fused_computation.8 | convolution fusion | flops 543158272 | bytes 10567680 | tf_op jit(solution)/shard_map/qngd,knd->ngqk/dot_general | solution.py:38
  158.6 2.1 %fusion.1 = (f32[8,4,128]{2,1,0:T(4,128)S(1)}, f32[8,512,128,4]{2,1,3,0:T(8,128)S(1)}) fusion(pred[128,512]{0,1:T(8,128)(4,1)S(1)} %get-tuple-element.45, bf16[128,8,4,128]{3,2,1,0:T(4,128)(2,1)S(1)} %reshape.261, bf16[512,8,256]{0,2,1:T(8,128)(2,1)S(1)} %bitcast.142), kind=kOutput, calls=%fused_computation.9 | convolution fusion | flops 543158272 | bytes 10567680 | tf_op jit(solution)/shard_map/qngd,knd->ngqk/dot_general | solution.py:38
  160.7 2.2 %fusion.11 = f32[8,4,128,128]{2,3,1,0:T(8,128)S(1)} fusion(bf16[512,8,256]{0,2,1:T(8,128)(2,1)S(1)} %bitcast.145, f32[8,512,128,4]{2,1,3,0:T(8,128)S(1)} %get-tuple-element.50, f32[8,4,128]{2,1,0:T(4,128)S(1)} %get-tuple-element.44, pred[128,512]{0,1:T(8,128)(4,1)S(1)} %get-tuple-element.46), kind=kOutput, calls=%fused_computation.31 | convolution fusion | flops 547356672 | bytes 11616256 | tf_op jit(solution)/shard_map/ngqk,knd->ngqd/dot_general | solution.py:53
  162.9 4.5 %convert_reduce_fusion = (f32[8,4,128]{2,1,0:T(4,128)S(1)}, f32[8,4,128]{2,1,0:T(4,128)S(1)}) fusion(f32[8,4,128]{2,1,0:T(4,128)S(1)} %get-tuple-element.43, f32[8,512,128,4]{2,1,3,0:T(8,128)S(1)} %get-tuple-element.48, pred[128,512]{0,1:T(8,128)(4,1)S(1)} %get-tuple-element.45, f32[8,4,128]{2,1,0:T(4,128)S(1)} %get-tuple-element.44, ...), kind=kLoop, calls=%fused_computation.4 | loop fusion | flops 29351936 | bytes 16973824 | tf_op jit(solution)/shard_map/reduce_sum | solution.py:52
  167.4 2.5 %fusion.4 = bf16[128,8,4,128]{0,3,2,1:T(8,128)(2,1)S(1)} fusion(f32[8,4,128,128]{2,3,1,0:T(8,128)S(1)} %fusion.11, bf16[512,8,256]{0,2,1:T(8,128)(2,1)S(1)} %bitcast.143, f32[128,8,4]{0,2,1:T(4,128)S(1)} %get-tuple-element.38, f32[128,8,4]{0,2,1:T(4,128)S(1)} %get-tuple-element.39, f32[128,8,4]{0,2,1:T(4,128)S(1)} %get-tuple-element.42, ...), kind=kOutput, calls=%fused_computation.14 | convolution fusion | flops 549978112 | bytes 12713984 | tf_op jit(solution)/shard_map/ngqk,knd->ngqd/dot_general | solution.py:53
  169.9 1.3 copy.33
  171.2 3.1 %copy.55 = bf16[32,128,256]{2,1,0:T(8,128)(2,1)} copy(bf16[32,128,256]{2,1,0:T(8,128)(2,1)} %collective-permute-done) | data formatting | bytes 4194304
  (30 shorter events, 0.4 us)
Async XLA Ops:
  7.2 3.6 %copy-start = (bf16[32,128,256]{2,1,0:T(8,128)(2,1)S(1)}, bf16[32,128,256]{2,1,0:T(8,128)(2,1)}, u32[]{:S(2)}) copy-start(bf16[32,128,256]{2,1,0:T(8,128)(2,1)} %param.14) | copy-start | bytes 6291460
  7.2 5.6 %copy-start.3 = (s32[1,32]{1,0:T(1,128)S(1)}, s32[1,32]{1,0:T(1,128)}, u32[]{:S(2)}) copy-start(s32[1,32]{1,0:T(1,128)} %param.15) | copy-start | bytes 388
  7.2 146.9 %all-gather.4.cloned.1.call-start = ((), (), s32[]{:S(2)}) async-start(), calls=%async_computation | async-start | bytes 4718592 | tf_op jit(solution)/shard_map/all_gather | solution.py:27
  16.0 138.0 %collective-permute-start = (bf16[32,128,256]{2,1,0:T(8,128)(2,1)}, bf16[32,128,256]{2,1,0:T(8,128)(2,1)}, u32[]{:S(2)}, u32[]{:S(2)}) collective-permute-start(bf16[32,128,256]{2,1,0:T(8,128)(2,1)} %select_select_fusion), channel_id=1, source_target_pairs={{248,0},{0,8},{8,16},{16,24},{24,32},{32,40},{40,48},{48,56},{56,6... | collective-permute-start | bytes 6291464 | tf_op jit(solution)/shard_map/ppermute | solution.py:16
  19.4 4.1 %copy-start.4 = (s32[32]{0:T(128)S(1)}, s32[32]{0:T(128)}, u32[]{:S(2)}) copy-start(s32[32]{0:T(128)} %param.13) | copy-start | bytes 388
  19.5 6.7 %copy-start.1 = (bf16[1,512]{1,0:T(2,128)(2,1)S(1)}, bf16[1,512]{1,0:T(2,128)(2,1)}, u32[]{:S(2)}) copy-start(bf16[1,512]{1,0:T(2,128)(2,1)} %param.11) | copy-start | bytes 3076
  19.5 90.9 %copy-start.2 = (bf16[1,256]{1,0:T(2,128)(2,1)S(1)}, bf16[1,256]{1,0:T(2,128)(2,1)}, u32[]{:S(2)}) copy-start(bf16[1,256]{1,0:T(2,128)(2,1)} %param.12) | copy-start | bytes 1540
Sparse Core Ops, SparseCore 0:
  10.4 40.1 all-gather.3
where the time goes:
time: 182 us; the launch traced here: 181 us
  blocking collectives  126 us (69%)
  between operations  16.8 us (9%)
  local copies, waits for them, and re-layouts  15.6 us (9%)
  other arithmetic  11.5 us (6%)
  matrix products  9.69 us (5%)
    all_gather x1, blocking collectives, decode_attention(): lax.all_gather(decode_queries, 'dp', axis=0, tiled=True)  84.3 us
    all_gather x1, blocking collectives, decode_attention(): lax.all_gather(decode_key_values, 'dp', axis=0, tiled=True)  41.7 us
    unnamed x14, local copies, waits for them, and re-layouts  7.25 us
    dot_general x2, matrix products, keys_attention(): jnp.einsum('ngqk,knd->ngqd', weights, key_block[:, :, HEAD_SIZE:], prefer...  4.67 us
    reduce_sum x1, other arithmetic, keys_attention(): jnp.sum(weights, axis=-1, dtype=jnp.float32)  4.47 us
    dot_general x2, matrix products, keys_attention(): jnp.einsum('qngd,knd->ngqk', query_rows, key_block[:, :, :HEAD_SIZE], pre...  4.16 us
  transfers between devices with their start and end apart: 2, of which 0 were waited for; matrix products, arithmetic and copies ran while one was open for 8% of the time, Pallas kernels for 0%

commit v1 on v0

--- a/solution.py
+++ b/solution.py
@@ -1,3 +1,4 @@
+import functools
 import math
 import jax
 import jax.numpy as jnp
@@ -8,6 +9,16 @@
 KV_HEAD_COUNT = 8
 HEAD_SIZE = 128
 NEG_FILL = -1e30
+
+
+def _form_hubs(local, mesh_dim):
+    upper = lax.axis_size(mesh_dim)
+    clean = jnp.stack([local] * upper, axis=0)
+    block_next = lax.all_to_all(clean, mesh_dim, 0, 0)
+    return jnp.concatenate(block_next, axis=0)
+
+
+put_the_cycles = functools.partial(_form_hubs, mesh_dim="dp")
 
 
 def passed_along(block, axis, distance):
@@ -72,7 +83,7 @@
     kv_local = decode_key_values.shape[1] // (2 * HEAD_SIZE)
     group_extent = QUERY_HEADS // KV_HEAD_COUNT
     query_all, pair_all = (
-        lax.all_gather(decode_queries, "dp", axis=0, tiled=True),
+        put_the_cycles(decode_queries),
         lax.all_gather(decode_key_values, "dp", axis=0, tiled=True),
     )
     total_rows = query_all.shape[0]

time: 182 us -> 150 us (0.82)
  blocking collectives: 126 us -> 76.1 us
  starting transfers between devices: 1.61 us -> 13.3 us
  other arithmetic: 11.5 us -> 14 us
  matrix products: 9.69 us -> 12.1 us
    all_gather x1 -> x0, blocking collectives: 84.3 us -> none  [decode_attention(): lax.all_gather(decode_queries, 'dp', axis=0, tiled=True)]
    all_gather x1, blocking collectives: 41.7 us -> 76.1 us  [decode_attention(): lax.all_gather(decode_key_values, 'dp', axis=0, tiled=True)]
    all_to_all x0 -> x1, starting transfers between devices: none -> 11.5 us  [_form_hubs(): block_next = lax.all_to_all(clean, mesh_dim, 0, 0)]
  transfers between devices with their start and end apart: 2 -> 3, of which waited for: 0 -> 0; matrix products, arithmetic and copies ran while one was open for 8% -> 14% of each run, Pallas kernels for 0% -> 0%
where the time goes in v1:
time: 150 us; the launch traced here: 149 us
  blocking collectives  76.1 us (51%)
  local copies, waits for them, and re-layouts  16.8 us (11%)
  between operations  16.8 us (11%)
  other arithmetic  14 us (9%)
  starting transfers between devices  13.3 us (9%)
  matrix products  12.1 us (8%)
    all_gather x1, blocking collectives, decode_attention(): lax.all_gather(decode_key_values, 'dp', axis=0, tiled=True)  76.1 us
    all_to_all x1, starting transfers between devices, _form_hubs(): block_next = lax.all_to_all(clean, mesh_dim, 0, 0)  11.5 us
    unnamed x14, local copies, waits for them, and re-layouts  7.88 us
    dot_general x2, matrix products, keys_attention(): jnp.einsum('ngqk,knd->ngqd', weights, key_block[:, :, HEAD_SIZE:], prefer...  4.67 us
    reduce_sum x1, other arithmetic, keys_attention(): jnp.sum(weights, axis=-1, dtype=jnp.float32)  4.47 us
    dot_general x2, matrix products, keys_attention(): jnp.einsum('qngd,knd->ngqk', query_rows, key_block[:, :, :HEAD_SIZE], pre...  4.15 us
    select_n x1, other arithmetic, move_pages(): page_rows = jnp.where(live_pages, page_rows, jnp.zeros_like(page_rows))  3.32 us
  transfers between devices with their start and end apart: 3, of which 0 were waited for; matrix products, arithmetic and copies ran while one was open for 14% of the time, Pallas kernels for 0%

profile of v1, /device:TPU:6, one launch (start us, length us, event | category | flops | bytes accessed | tf_op | source)
XLA Modules:
  0.0 149.1 jit_solution(9238252749632036468)
XLA Ops:
  7.2 2.2 %copy.26 = bf16[128,2048]{0,1:T(8,128)(2,1)} copy(bf16[128,2048]{1,0:T(8,128)(2,1)} %param.10) | data formatting | bytes 1048576 | tf_op args[1]
  9.4 0.7 reduce.6
  10.7 0.8 reduce.9
  11.5 0.6 reshape.358
  12.1 11.5 %all-to-all-start = ((bf16[32,2,256]{2,1,0:T(2,128)(2,1)}), bf16[32,2,256]{2,1,0:T(2,128)(2,1)S(1)}, u32[]{:S(2)}, u32[]{:S(2)}) async-start(bf16[32,2,256]{2,1,0:T(2,128)(2,1)} %reshape.358), calls=%async_computation | async-start | bytes 65536 | tf_op jit(solution)/shard_map/all_to_all | solution.py:17
  24.3 0.7 fusion.23
  25.0 2.0 %gather_fusion.1 = bf16[32,128,256]{2,1,0:T(8,128)(2,1)} fusion(bf16[32,128,256]{2,1,0:T(8,128)(2,1)S(1)} %copy-done, s32[1024]{0:T(1024)S(1)} %pad_clamp_fusion), kind=kCustom, calls=%fused_computation.1 | custom fusion | bytes 4194432 | tf_op jit(solution)/shard_map/jit(_take)/gather | solution.py:155
  27.0 3.3 %select_select_fusion = bf16[32,128,256]{2,1,0:T(8,128)(2,1)} fusion(bf16[32,128,256]{2,1,0:T(8,128)(2,1)} %gather_fusion.1, pred[32]{0:T(512)(128)(4,1)S(1)} %get-tuple-element.57, pred[32]{0:T(512)(128)(4,1)S(1)} %get-tuple-element.58), kind=kLoop, calls=%fused_computation.17 | loop fusion | flops 2097152 | bytes 4194368 | tf_op jit(solution)/shard_map/jit(_where)/select_n | solution.py:160
  30.3 1.8 %collective-permute-start = (bf16[32,128,256]{2,1,0:T(8,128)(2,1)}, bf16[32,128,256]{2,1,0:T(8,128)(2,1)}, u32[]{:S(2)}, u32[]{:S(2)}) collective-permute-start(bf16[32,128,256]{2,1,0:T(8,128)(2,1)} %select_select_fusion), channel_id=1, source_target_pairs={{248,0},{0,8},{8,16},{16,24},{24,32},{32,40},{40,48},{48,56},{56,6... | collective-permute-start | bytes 6291464 | tf_op jit(solution)/shard_map/ppermute | solution.py:27
  32.1 1.8 %reshape.267 = bf16[128,8,4,128]{3,2,1,0:T(4,128)(2,1)S(1)} reshape(bf16[128,4096]{1,0:T(8,128)(2,1)} %param.9) | data formatting | bytes 2097152 | tf_op jit(solution)/shard_map/reshape | solution.py:33
  33.9 2.0 %gather_fusion = bf16[32,128,256]{2,1,0:T(8,128)(2,1)} fusion(bf16[32,128,256]{2,1,0:T(8,128)(2,1)S(1)} %copy-done, s32[1024]{0:T(1024)S(1)} %pad_clamp_fusion.1), kind=kCustom, calls=%fused_computation | custom fusion | bytes 4194432 | tf_op jit(solution)/shard_map/jit(_take)/gather | solution.py:101
  35.9 0.6 fusion.22
  38.5 76.1 %all-gather = bf16[32,1,256]{2,1,0:T(2,128)(2,1)S(1)} all-gather(bf16[1,1,256]{2,1,0:T(2,128)(2,1)S(1)} %bitcast.147), channel_id=1, replica_groups=mesh['dp'=32,'seq'=8] {'dp'}, dimensions={0}, use_global_device_ids=true | all-gather | bytes 16896 | tf_op jit(solution)/shard_map/all_gather | solution.py:87
  114.8 2.9 %broadcast_select_fusion = bf16[1,4096,1,256]{3,1,2,0:T(8,128)(2,1)} fusion(bf16[1,4096,1,256]{3,1,2,0:T(8,128)(2,1)} %bitcast.140, pred[4096]{0:T(1024)(128)(4,1)S(1)} %broadcast_bitcast_fusion), kind=kLoop, calls=%fused_computation.18 | loop fusion | flops 1048576 | bytes 4198400 | tf_op jit(solution)/shard_map/jit(_take)/select_n | solution.py:101
  117.8 1.7 %fusion.30 = (f32[4]{0:T(128)S(1)}, f32[4,4096]{1,0:T(4,128)S(1)}) fusion(bf16[1,4096,1,256]{3,1,2,0:T(8,128)(2,1)} %broadcast_select_fusion, bf16[512]{0:T(512)(128)(2,1)S(1)} %fusion.19, pred[4096]{0:T(1024)(128)(4,1)S(1)} %iota_compare_fusion.1), kind=kOutput, calls=%fused_computation.78 | convolution fusion | flops 4243452 | bytes 1119248 | tf_op jit(solution)/shard_map/rngd,rtnd->rngt/dot_general | solution.py:106
  119.9 1.5 fusion.8
  122.0 2.5 %fusion.29 = (bf16[512,2048]{0,1:T(8,128)(2,1)S(1)}, bf16[512,2048]{0,1:T(8,128)(2,1)S(1)}) fusion(bf16[1024,2048]{0,1:T(8,128)(2,1)} %all-gather.3.cloned.1.call-done), kind=kLoop, calls=%fused_computation.77 | loop fusion | bytes 8388608 | tf_op jit(solution)/shard_map/slice | solution.py:47
  124.5 2.1 %fusion = (f32[8,4,128]{2,1,0:T(4,128)S(1)}, f32[8,512,128,4]{2,1,3,0:T(8,128)S(1)}) fusion(pred[128,512]{0,1:T(8,128)(4,1)S(1)} %get-tuple-element.46, bf16[128,8,4,128]{3,2,1,0:T(4,128)(2,1)S(1)} %reshape.267, bf16[512,8,256]{0,2,1:T(8,128)(2,1)S(1)} %bitcast.143), kind=kOutput, calls=%fused_computation.8 | convolution fusion | flops 543158272 | bytes 10567680 | tf_op jit(solution)/shard_map/qngd,knd->ngqk/dot_general | solution.py:49
  126.6 2.1 %fusion.1 = (f32[8,4,128]{2,1,0:T(4,128)S(1)}, f32[8,512,128,4]{2,1,3,0:T(8,128)S(1)}) fusion(pred[128,512]{0,1:T(8,128)(4,1)S(1)} %get-tuple-element.45, bf16[128,8,4,128]{3,2,1,0:T(4,128)(2,1)S(1)} %reshape.267, bf16[512,8,256]{0,2,1:T(8,128)(2,1)S(1)} %bitcast.141), kind=kOutput, calls=%fused_computation.9 | convolution fusion | flops 543158272 | bytes 10567680 | tf_op jit(solution)/shard_map/qngd,knd->ngqk/dot_general | solution.py:49
  128.7 2.2 %fusion.11 = f32[8,4,128,128]{2,3,1,0:T(8,128)S(1)} fusion(bf16[512,8,256]{0,2,1:T(8,128)(2,1)S(1)} %bitcast.144, f32[8,512,128,4]{2,1,3,0:T(8,128)S(1)} %get-tuple-element.50, f32[8,4,128]{2,1,0:T(4,128)S(1)} %get-tuple-element.44, pred[128,512]{0,1:T(8,128)(4,1)S(1)} %get-tuple-element.46), kind=kOutput, calls=%fused_computation.31 | convolution fusion | flops 547356672 | bytes 11616256 | tf_op jit(solution)/shard_map/ngqk,knd->ngqd/dot_general | solution.py:64
  130.8 4.5 %convert_reduce_fusion = (f32[8,4,128]{2,1,0:T(4,128)S(1)}, f32[8,4,128]{2,1,0:T(4,128)S(1)}) fusion(f32[8,4,128]{2,1,0:T(4,128)S(1)} %get-tuple-element.43, f32[8,512,128,4]{2,1,3,0:T(8,128)S(1)} %get-tuple-element.48, pred[128,512]{0,1:T(8,128)(4,1)S(1)} %get-tuple-element.45, f32[8,4,128]{2,1,0:T(4,128)S(1)} %get-tuple-element.44, ...), kind=kLoop, calls=%fused_computation.4 | loop fusion | flops 29351936 | bytes 16973824 | tf_op jit(solution)/shard_map/reduce_sum | solution.py:63
  135.3 2.5 %fusion.4 = bf16[128,8,4,128]{0,3,2,1:T(8,128)(2,1)S(1)} fusion(f32[8,4,128,128]{2,3,1,0:T(8,128)S(1)} %fusion.11, bf16[512,8,256]{0,2,1:T(8,128)(2,1)S(1)} %bitcast.142, f32[128,8,4]{0,2,1:T(4,128)S(1)} %get-tuple-element.38, f32[128,8,4]{0,2,1:T(4,128)S(1)} %get-tuple-element.39, f32[128,8,4]{0,2,1:T(4,128)S(1)} %get-tuple-element.42, ...), kind=kOutput, calls=%fused_computation.14 | convolution fusion | flops 549978112 | bytes 12713984 | tf_op jit(solution)/shard_map/ngqk,knd->ngqd/dot_general | solution.py:64
  137.8 1.3 copy.33
  139.2 3.1 %copy.55 = bf16[32,128,256]{2,1,0:T(8,128)(2,1)} copy(bf16[32,128,256]{2,1,0:T(8,128)(2,1)} %collective-permute-done) | data formatting | bytes 4194304
  (35 shorter events, 2.0 us)
Async XLA Ops:
  7.2 17.8 %copy-start = (bf16[32,128,256]{2,1,0:T(8,128)(2,1)S(1)}, bf16[32,128,256]{2,1,0:T(8,128)(2,1)}, u32[]{:S(2)}) copy-start(bf16[32,128,256]{2,1,0:T(8,128)(2,1)} %param.14) | copy-start | bytes 6291460
  7.2 19.8 %copy-start.2 = (s32[1,32]{1,0:T(1,128)S(1)}, s32[1,32]{1,0:T(1,128)}, u32[]{:S(2)}) copy-start(s32[1,32]{1,0:T(1,128)} %param.15) | copy-start | bytes 388
  7.2 114.8 %all-gather.3.cloned.1.call-start = ((), (), s32[]{:S(2)}) async-start(), calls=%async_computation.1 | async-start | bytes 4718592 | tf_op jit(solution)/shard_map/all_gather | solution.py:38
  12.1 105.6 %all-to-all-start = ((bf16[32,2,256]{2,1,0:T(2,128)(2,1)}), bf16[32,2,256]{2,1,0:T(2,128)(2,1)S(1)}, u32[]{:S(2)}, u32[]{:S(2)}) async-start(bf16[32,2,256]{2,1,0:T(2,128)(2,1)} %reshape.358), calls=%async_computation | async-start | bytes 65536 | tf_op jit(solution)/shard_map/all_to_all | solution.py:17
  30.3 5.6 %copy-start.3 = (s32[32]{0:T(128)S(1)}, s32[32]{0:T(128)}, u32[]{:S(2)}) copy-start(s32[32]{0:T(128)} %param.13) | copy-start | bytes 388
  30.3 8.2 %copy-start.1 = (bf16[1,256]{1,0:T(2,128)(2,1)S(1)}, bf16[1,256]{1,0:T(2,128)(2,1)}, u32[]{:S(2)}) copy-start(bf16[1,256]{1,0:T(2,128)(2,1)} %param.12) | copy-start | bytes 1540
  30.3 91.7 %collective-permute-start = (bf16[32,128,256]{2,1,0:T(8,128)(2,1)}, bf16[32,128,256]{2,1,0:T(8,128)(2,1)}, u32[]{:S(2)}, u32[]{:S(2)}) collective-permute-start(bf16[32,128,256]{2,1,0:T(8,128)(2,1)} %select_select_fusion), channel_id=1, source_target_pairs={{248,0},{0,8},{8,16},{16,24},{24,32},{32,40},{40,48},{48,56},{56,6... | collective-permute-start | bytes 6291464 | tf_op jit(solution)/shard_map/ppermute | solution.py:27
Sparse Core Ops, SparseCore 0:
  10.4 40.3 all-gather.2
